TPU v7x, 512 devices: a whole 4x8x8 slice. The times are simulated.
512 devices in a mesh: dp: 8 (over x, core), ctx: 64 (over y, z).
Axes of the slice: x: 4, y: 8, z: 8, core: 2. Of those that a mesh axis runs over, the one named last changes fastest.
Arguments:
- queries: bfloat16 [16, 4096, 2048], P('dp', 'ctx'), may hold values from -52 to 52
- key_rows: bfloat16 [16, 4096, 2048], P('dp', 'ctx'), may hold values from -4 to 4
- value_rows: bfloat16 [16, 4096, 2048], P('dp', 'ctx'), may hold values from -6 to 6
- out_grad: bfloat16 [16, 4096, 2048], P('dp', 'ctx'), may hold values from -64 to 64
- level_slope: float32 [16], replicated, may hold values from -0.5 to 0.5
Outputs:
- query_grad: bfloat16 [16, 4096, 2048], P('dp', 'ctx')
- key_grad: bfloat16 [16, 4096, 2048], P('dp', 'ctx')
- value_grad: bfloat16 [16, 4096, 2048], P('dp', 'ctx')
- slope_grad: float32 [16], replicated
All inputs are finite; a program needn't handle non-finite values.
Results may differ from a plain program's by a relative error of at most 0.0075.
Values may be sent and summed in bfloat16 or wider, within the bound.
A program may use at most 64 MiB of HBM per device.

v0:
```python
import math
import jax
import jax.numpy as jnp
from jax import lax
from jax.sharding import PartitionSpec as P


def as_sent(x):
    return jax.tree.map(lambda a: a.astype(jnp.bfloat16) if a.dtype == jnp.float32 else a, x)


def from_partner(value, axis, apart):
    mask = 2**apart
    pairs = [(source, source ^ mask) for source in range(lax.axis_size(axis))]
    return lax.ppermute(value, axis, pairs)


def pair_mean(cells):
    shaped = cells.reshape(cells.shape[:-2] + (cells.shape[-2] // 2, 2, cells.shape[-1])).astype(
        jnp.float32
    )
    return ((shaped[..., 0, :] + shaped[..., 1, :]) * 0.5).astype(jnp.bfloat16)


def merge_level(own_pair, other_pair, flag):
    merged = []
    for own_part, other_part in zip(own_pair, other_pair):
        own_small = pair_mean(own_part)
        other_small = pair_mean(other_part)
        merged.append(
            jnp.where(
                flag == 1,
                jnp.concatenate([other_small, own_small], axis=1),
                jnp.concatenate([own_small, other_small], axis=1),
            )
        )
    return tuple(merged)


def to_heads(rows, heads):
    seqs, count, width = rows.shape
    return jnp.transpose(rows.reshape(seqs, count, heads, width // heads), (0, 2, 1, 3))


def from_heads(split):
    seqs, heads, count, head = split.shape
    return jnp.transpose(split, (0, 2, 1, 3)).reshape(seqs, count, heads * head)


def product(form, left, right):
    return jnp.einsum(form, left, right, preferred_element_type=jnp.float32)


def attend(query_four, key_four, value_four, grad_four, level_slope, block):
    head = query_four.shape[3]
    key_count = key_four.shape[2]
    scale = 1.0 / math.sqrt(head)
    column = jnp.arange(key_count, dtype=jnp.int32)
    level_of = column // block - 1
    sibling = jnp.maximum(level_of, 0)
    multiple = jnp.where(level_of < 0, 1.0, jnp.exp2(sibling.astype(jnp.float32)))
    bias = level_slope[:, None] * sibling.astype(jnp.float32)[None, :]
    raw = product("shqd,shkd->shqk", query_four, key_four)
    scores = raw * scale + bias[None, :, None, :]
    top = jnp.max(scores, axis=-1, keepdims=True)
    weights = multiple[None, None, None, :] * jnp.exp(scores - top)
    probs = weights / jnp.sum(weights, axis=-1, keepdims=True)
    probs_low = probs.astype(jnp.bfloat16)
    output = product("shqk,shkd->shqd", probs_low, value_four)
    delta = jnp.sum(grad_four.astype(jnp.float32) * output, axis=-1)
    upstream = product("shqd,shkd->shqk", grad_four, value_four)
    dscore = probs * (upstream - delta[..., None])
    slope_part = jnp.sum(dscore * sibling.astype(jnp.float32)[None, None, None, :], axis=(0, 2, 3))
    dscore_low = dscore.astype(jnp.bfloat16)
    query_part = product("shqk,shkd->shqd", dscore_low, key_four) * scale
    key_part = product("shqk,shqd->shkd", dscore_low, query_four) * scale
    value_part = product("shqk,shqd->shkd", probs_low, grad_four)
    return (query_part, key_part, value_part, slope_part)


def split_level(grad_now, direct, flag, level, block):
    half = block // 2
    lower_src = grad_now[:, :, :half]
    upper_src = grad_now[:, :, half:]
    own_src = jnp.where(flag == 1, upper_src, lower_src)
    other_src = jnp.where(flag == 1, lower_src, upper_src)
    own_half = jnp.repeat(own_src, 2, axis=2) * 0.5
    other_half = jnp.repeat(other_src, 2, axis=2) * 0.5
    sent = (other_half + direct[:, :, (level + 1) * block : (level + 2) * block]).astype(
        jnp.bfloat16
    )
    return (own_half, sent)


def shards(queries, key_rows, value_rows, out_grad, level_slope):
    seqs, block, width = queries.shape
    heads = level_slope.shape[0]
    ctx_count = lax.axis_size("ctx")
    levels = ctx_count.bit_length() - 1
    position = lax.axis_index("ctx")
    bit_list = [position // 2**level % 2 for level in range(levels)]
    own_pair = (key_rows, value_rows)
    partners = []
    for level in range(levels - 2):
        other_pair = jax.tree.map(
            lambda part, own: part.astype(own.dtype),
            from_partner(as_sent(own_pair), "ctx", level),
            own_pair,
        )
        partners.append(other_pair)
        own_pair = merge_level(own_pair, other_pair, bit_list[level])
    for level in range(levels - 2, levels):
        other_pair = jax.tree.map(
            lambda part, own: part.astype(own.dtype),
            from_partner(as_sent(own_pair), "ctx", level),
            own_pair,
        )
        partners.append(other_pair)
        if level + 1 < levels:
            own_pair = merge_level(own_pair, other_pair, bit_list[level])
    key_set = jnp.concatenate(
        [to_heads(key_rows, heads)] + [to_heads(pair[0], heads) for pair in partners], axis=2
    )
    value_set = jnp.concatenate(
        [to_heads(value_rows, heads)] + [to_heads(pair[1], heads) for pair in partners], axis=2
    )
    query_four = to_heads(queries, heads)
    grad_four = to_heads(out_grad, heads)
    query_part, key_part, value_part, slope_part = attend(
        query_four, key_set, value_set, grad_four, level_slope, block
    )
    slope_grad = lax.psum(slope_part, ("dp", "ctx"))
    head = width // heads
    grad_keys = jnp.zeros((seqs, heads, block, head), jnp.float32)
    grad_values = jnp.zeros((seqs, heads, block, head), jnp.float32)
    for level in reversed(range(levels)):
        own_keys, sent_keys = split_level(grad_keys, key_part, bit_list[level], level, block)
        own_values, sent_values = split_level(
            grad_values, value_part, bit_list[level], level, block
        )
        back_keys, back_values = from_partner((sent_keys, sent_values), "ctx", level)
        grad_keys = own_keys + back_keys.astype(jnp.float32)
        grad_values = own_values + back_values.astype(jnp.float32)
    key_grad = from_heads((grad_keys + key_part[:, :, :block]).astype(jnp.bfloat16))
    value_grad = from_heads((grad_values + value_part[:, :, :block]).astype(jnp.bfloat16))
    return (from_heads(query_part.astype(jnp.bfloat16)), key_grad, value_grad, slope_grad)


def solution(mesh):
    placed = (
        P("dp", "ctx", None),
        P("dp", "ctx", None),
        P("dp", "ctx", None),
        P("dp", "ctx", None),
        P(),
    )
    return jax.shard_map(
        shards,
        mesh=mesh,
        in_specs=placed,
        out_specs=(P("dp", "ctx", None), P("dp", "ctx", None), P("dp", "ctx", None), P()),
        check_vma=False,
    )
```

profile of v0, /device:TPU:1, one launch (start us, length us, event | category | flops | bytes accessed | tf_op | source)
XLA Modules:
  0.0 589.4 jit_solution(14422107451718763266)
XLA Ops:
  0.7 5.0 collective-permute-start
  5.6 1.9 collective-permute-start.6
  7.7 1.6 copy.84
  9.3 1.6 copy.119
  10.9 2.0 fusion.33
  15.2 9.6 %collective-permute-done.6 = bf16[2,64,2048]{2,1,0:T(8,128)(2,1)} collective-permute-done((bf16[2,64,2048]{2,1,0:T(8,128)(2,1)}, bf16[2,64,2048]{2,1,0:T(8,128)(2,1)}, u32[]{:S(2)}, u32[]{:S(2)}) %collective-permute-start.6) | collective-permute-done | bytes 524320 | tf_op jit(solution)/shard_map/ppermute | solution.py:15
  24.8 1.6 copy.116
  26.8 1.6 copy.82
  30.0 9.8 %collective-permute-start.1 = (bf16[2,64,2048]{2,0,1:T(2,128)(2,1)S(1)}, bf16[2,64,2048]{2,0,1:T(2,128)(2,1)S(1)}, u32[]{:S(2)}, u32[]{:S(2)}) collective-permute-start(bf16[2,64,2048]{2,0,1:T(2,128)(2,1)S(1)} %broadcast_select_fusion.9), channel_id=1, source_target_pairs={{0,2},{1,3},{2,0},{3,1},{4,6},{5,7},{6,4},{7,5},{8,10},{9,11},{10,... | collective-permute-start | bytes 1572872 | tf_op jit(solution)/shard_map/ppermute | solution.py:15
  41.5 1.9 collective-permute-start.7
  44.0 2.0 fusion.32
  46.0 2.0 fusion.29
  48.0 25.8 %collective-permute-done.1 = bf16[2,64,2048]{2,0,1:T(2,128)(2,1)S(1)} collective-permute-done((bf16[2,64,2048]{2,0,1:T(2,128)(2,1)S(1)}, bf16[2,64,2048]{2,0,1:T(2,128)(2,1)S(1)}, u32[]{:S(2)}, u32[]{:S(2)}) %collective-permute-start.1) | collective-permute-done | bytes 524320 | tf_op jit(solution)/shard_map/ppermute | solution.py:15
  76.5 8.4 %collective-permute-start.2 = (bf16[2,64,2048]{2,0,1:T(2,128)(2,1)S(1)}, bf16[2,64,2048]{2,0,1:T(2,128)(2,1)S(1)}, u32[]{:S(2)}, u32[]{:S(2)}) collective-permute-start(bf16[2,64,2048]{2,0,1:T(2,128)(2,1)S(1)} %broadcast_select_fusion.7), channel_id=1, source_target_pairs={{0,4},{1,5},{2,6},{3,7},{4,0},{5,1},{6,2},{7,3},{8,12},{9,13},{10,... | collective-permute-start | bytes 1572872 | tf_op jit(solution)/shard_map/ppermute | solution.py:15
  87.3 1.9 broadcast_select_fusion.6
  89.3 30.1 %collective-permute-start.8 = (bf16[2,64,2048]{2,0,1:T(2,128)(2,1)}, bf16[2,64,2048]{2,0,1:T(2,128)(2,1)S(1)}, u32[]{:S(2)}, u32[]{:S(2)}) collective-permute-start(bf16[2,64,2048]{2,0,1:T(2,128)(2,1)} %broadcast_select_fusion.6), channel_id=1, source_target_pairs={{0,4},{1,5},{2,6},{3,7},{4,0},{5,1},{6,2},{7,3},{8,12},{9,13},{10,... | collective-permute-start | bytes 1572872 | tf_op jit(solution)/shard_map/ppermute | solution.py:15
  120.5 2.1 bitcast_dynamic-update-slice_fusion.9
  123.9 1.6 convert.39
  128.0 3.2 collective-permute-start.3
  132.2 9.6 %collective-permute-done.8 = bf16[2,64,2048]{2,0,1:T(2,128)(2,1)S(1)} collective-permute-done((bf16[2,64,2048]{2,0,1:T(2,128)(2,1)}, bf16[2,64,2048]{2,0,1:T(2,128)(2,1)S(1)}, u32[]{:S(2)}, u32[]{:S(2)}) %collective-permute-start.8) | collective-permute-done | bytes 524320 | tf_op jit(solution)/shard_map/ppermute | solution.py:15
  142.8 1.9 broadcast_select_fusion.4
  144.7 3.6 collective-permute-start.9
  149.4 2.1 bitcast_dynamic-update-slice_fusion.8
  152.9 1.6 convert.41
  157.1 4.2 collective-permute-start.4
  163.2 1.9 broadcast_select_fusion.2
  165.2 2.0 collective-permute-start.10
  168.3 2.1 bitcast_dynamic-update-slice_fusion.7
  171.7 1.6 convert.43
  173.7 22.1 %collective-permute-done.4 = bf16[2,64,2048]{2,0,1:T(2,128)(2,1)S(1)} collective-permute-done((bf16[2,64,2048]{2,0,1:T(2,128)(2,1)S(1)}, bf16[2,64,2048]{2,0,1:T(2,128)(2,1)S(1)}, u32[]{:S(2)}, u32[]{:S(2)}) %collective-permute-start.4) | collective-permute-done | bytes 524320 | tf_op jit(solution)/shard_map/ppermute | solution.py:15
  196.8 1.9 broadcast_select_fusion.1
  198.8 6.3 %collective-permute-start.5 = (bf16[2,64,2048]{2,0,1:T(2,128)(2,1)}, bf16[2,64,2048]{2,0,1:T(2,128)(2,1)S(1)}, u32[]{:S(2)}, u32[]{:S(2)}) collective-permute-start(bf16[2,64,2048]{2,0,1:T(2,128)(2,1)} %broadcast_select_fusion.1), channel_id=1, source_target_pairs={{0,32},{1,33},{2,34},{3,35},{4,36},{5,37},{6,38},{7,39},{8,40},{9,... | collective-permute-start | bytes 1572872 | tf_op jit(solution)/shard_map/ppermute | solution.py:15
  205.0 2.2 collective-permute-done.10
  208.1 1.9 broadcast_select_fusion
  210.1 20.2 %collective-permute-start.11 = (bf16[2,64,2048]{2,0,1:T(2,128)(2,1)}, bf16[2,64,2048]{2,0,1:T(2,128)(2,1)S(1)}, u32[]{:S(2)}, u32[]{:S(2)}) collective-permute-start(bf16[2,64,2048]{2,0,1:T(2,128)(2,1)} %broadcast_select_fusion), channel_id=1, source_target_pairs={{0,32},{1,33},{2,34},{3,35},{4,36},{5,37},{6,38},{7,39},{8,40},{9,... | collective-permute-start | bytes 1572872 | tf_op jit(solution)/shard_map/ppermute | solution.py:15
  234.4 22.0 %collective-permute-done.11 = bf16[2,64,2048]{2,0,1:T(2,128)(2,1)S(1)} collective-permute-done((bf16[2,64,2048]{2,0,1:T(2,128)(2,1)}, bf16[2,64,2048]{2,0,1:T(2,128)(2,1)S(1)}, u32[]{:S(2)}, u32[]{:S(2)}) %collective-permute-start.11) | collective-permute-done | bytes 524320 | tf_op jit(solution)/shard_map/ppermute | solution.py:15
  257.7 3.7 fusion.31
  261.4 1.6 fusion.123
  263.0 1.9 fusion.28
  266.1 2.1 multiply_reduce_fusion
  269.1 5.7 collective-permute-start.18
  275.7 101.6 %psum.7 = f32[16]{0:T(128)} all-reduce(f32[16]{0:T(128)S(1)} %get-tuple-element.26), channel_id=1, replica_groups=mesh['dp'=8,'ctx'=64] {'dp','ctx'}, use_global_device_ids=true, to_apply=%region_4.5 | all-reduce | flops 16 | bytes 128 | tf_op jit(solution)/shard_map/psum | solution.py:132
  379.5 5.8 collective-permute-start.12
  387.2 1.9 collective-permute-start.19
  389.1 20.6 %collective-permute-done.12 = bf16[2,16,64,128]{3,2,1,0:T(8,128)(2,1)S(1)} collective-permute-done((bf16[2,16,64,128]{3,2,1,0:T(8,128)(2,1)S(1)}, bf16[2,16,64,128]{3,2,1,0:T(8,128)(2,1)S(1)}, u32[]{:S(2)}, u32[]{:S(2)}) %collective-permute-start.12) | collective-permute-done | bytes 524320 | tf_op jit(solution)/shard_map/ppermute | solution.py:15
  410.5 1.9 collective-permute-start.13
  412.4 30.1 %collective-permute-done.19 = bf16[2,16,64,128]{3,2,1,0:T(8,128)(2,1)S(1)} collective-permute-done((bf16[2,16,64,128]{3,2,1,0:T(8,128)(2,1)S(1)}, bf16[2,16,64,128]{3,2,1,0:T(8,128)(2,1)S(1)}, u32[]{:S(2)}, u32[]{:S(2)}) %collective-permute-start.19) | collective-permute-done | bytes 524320 | tf_op jit(solution)/shard_map/ppermute | solution.py:15
  443.8 2.4 collective-permute-start.20
  446.3 7.6 %collective-permute-done.13 = bf16[2,16,64,128]{3,2,1,0:T(8,128)(2,1)S(1)} collective-permute-done((bf16[2,16,64,128]{3,2,1,0:T(8,128)(2,1)S(1)}, bf16[2,16,64,128]{3,2,1,0:T(8,128)(2,1)S(1)}, u32[]{:S(2)}, u32[]{:S(2)}) %collective-permute-start.13) | collective-permute-done | bytes 524320 | tf_op jit(solution)/shard_map/ppermute | solution.py:15
  455.0 2.4 collective-permute-start.14
  457.5 7.5 %collective-permute-done.20 = bf16[2,16,64,128]{3,2,1,0:T(8,128)(2,1)S(1)} collective-permute-done((bf16[2,16,64,128]{3,2,1,0:T(8,128)(2,1)S(1)}, bf16[2,16,64,128]{3,2,1,0:T(8,128)(2,1)S(1)}, u32[]{:S(2)}, u32[]{:S(2)}) %collective-permute-start.20) | collective-permute-done | bytes 524320 | tf_op jit(solution)/shard_map/ppermute | solution.py:15
  466.3 5.2 collective-permute-start.21
  471.5 4.7 collective-permute-done.14
  477.5 5.2 collective-permute-start.15
  482.7 24.9 %collective-permute-done.21 = bf16[2,16,64,128]{3,2,1,0:T(8,128)(2,1)S(1)} collective-permute-done((bf16[2,16,64,128]{3,2,1,0:T(8,128)(2,1)S(1)}, bf16[2,16,64,128]{3,2,1,0:T(8,128)(2,1)S(1)}, u32[]{:S(2)}, u32[]{:S(2)}) %collective-permute-start.21) | collective-permute-done | bytes 524320 | tf_op jit(solution)/shard_map/ppermute | solution.py:15
  508.9 1.9 collective-permute-start.22
  510.8 8.1 %collective-permute-done.15 = bf16[2,16,64,128]{3,2,1,0:T(8,128)(2,1)S(1)} collective-permute-done((bf16[2,16,64,128]{3,2,1,0:T(8,128)(2,1)S(1)}, bf16[2,16,64,128]{3,2,1,0:T(8,128)(2,1)S(1)}, u32[]{:S(2)}, u32[]{:S(2)}) %collective-permute-start.15) | collective-permute-done | bytes 524320 | tf_op jit(solution)/shard_map/ppermute | solution.py:15
  520.2 2.2 collective-permute-start.16
  522.4 31.5 %collective-permute-done.22 = bf16[2,16,64,128]{3,2,1,0:T(8,128)(2,1)S(1)} collective-permute-done((bf16[2,16,64,128]{3,2,1,0:T(8,128)(2,1)S(1)}, bf16[2,16,64,128]{3,2,1,0:T(8,128)(2,1)S(1)}, u32[]{:S(2)}, u32[]{:S(2)}) %collective-permute-start.22) | collective-permute-done | bytes 524320 | tf_op jit(solution)/shard_map/ppermute | solution.py:15
  555.1 1.9 collective-permute-start.23
  557.0 8.1 %collective-permute-done.16 = bf16[2,16,64,128]{3,2,1,0:T(8,128)(2,1)S(1)} collective-permute-done((bf16[2,16,64,128]{3,2,1,0:T(8,128)(2,1)S(1)}, bf16[2,16,64,128]{3,2,1,0:T(8,128)(2,1)S(1)}, u32[]{:S(2)}, u32[]{:S(2)}) %collective-permute-start.16) | collective-permute-done | bytes 524320 | tf_op jit(solution)/shard_map/ppermute | solution.py:15
  566.4 1.9 collective-permute-start.17
  568.3 8.0 %collective-permute-done.23 = bf16[2,16,64,128]{3,2,1,0:T(8,128)(2,1)S(1)} collective-permute-done((bf16[2,16,64,128]{3,2,1,0:T(8,128)(2,1)S(1)}, bf16[2,16,64,128]{3,2,1,0:T(8,128)(2,1)S(1)}, u32[]{:S(2)}, u32[]{:S(2)}) %collective-permute-start.23) | collective-permute-done | bytes 524320 | tf_op jit(solution)/shard_map/ppermute | solution.py:15
  577.7 9.9 %collective-permute-done.17 = bf16[2,16,64,128]{3,2,1,0:T(8,128)(2,1)S(1)} collective-permute-done((bf16[2,16,64,128]{3,2,1,0:T(8,128)(2,1)S(1)}, bf16[2,16,64,128]{3,2,1,0:T(8,128)(2,1)S(1)}, u32[]{:S(2)}, u32[]{:S(2)}) %collective-permute-start.17) | collective-permute-done | bytes 524320 | tf_op jit(solution)/shard_map/ppermute | solution.py:15
  (145 shorter events, 55.8 us)
Async XLA Ops:
  0.6 262.4 %copy-start = (bf16[2,64,2048]{2,1,0:T(8,128)(2,1)S(1)}, bf16[2,64,2048]{2,1,0:T(8,128)(2,1)}, u32[]{:S(2)}) copy-start(bf16[2,64,2048]{2,1,0:T(8,128)(2,1)} %param.8) | copy-start | bytes 1572868
  0.6 12.2 %copy-start.5 = (bf16[2,64,2048]{2,1,0:T(8,128)(2,1)S(1)}, bf16[2,64,2048]{2,1,0:T(8,128)(2,1)}, u32[]{:S(2)}) copy-start(bf16[2,64,2048]{2,1,0:T(8,128)(2,1)} %param.7) | copy-start | bytes 1572868
  0.7 26.2 %collective-permute-start = (bf16[2,64,2048]{2,1,0:T(8,128)(2,1)}, bf16[2,64,2048]{2,1,0:T(8,128)(2,1)}, u32[]{:S(2)}, u32[]{:S(2)}) collective-permute-start(bf16[2,64,2048]{2,1,0:T(8,128)(2,1)} %param.6), channel_id=1, source_target_pairs={{0,1},{1,0},{2,3},{3,2},{4,5},{5,4},{6,7},{7,6},{8,9},{9,8},{10,11... | collective-permute-start | bytes 1572872 | tf_op jit(solution)/shard_map/ppermute | solution.py:15
  5.6 19.1 %collective-permute-start.6 = (bf16[2,64,2048]{2,1,0:T(8,128)(2,1)}, bf16[2,64,2048]{2,1,0:T(8,128)(2,1)}, u32[]{:S(2)}, u32[]{:S(2)}) collective-permute-start(bf16[2,64,2048]{2,1,0:T(8,128)(2,1)} %param.7), channel_id=1, source_target_pairs={{0,1},{1,0},{2,3},{3,2},{4,5},{5,4},{6,7},{7,6},{8,9},{9,8},{10,11... | collective-permute-start | bytes 1572872 | tf_op jit(solution)/shard_map/ppermute | solution.py:15
  7.7 7.0 %copy-start.7 = (f32[16]{0:T(128)S(1)}, f32[16]{0:T(128)}, u32[]{:S(2)}) copy-start(f32[16]{0:T(128)} %param.9) | copy-start | bytes 196
  30.0 43.8 %collective-permute-start.1 = (bf16[2,64,2048]{2,0,1:T(2,128)(2,1)S(1)}, bf16[2,64,2048]{2,0,1:T(2,128)(2,1)S(1)}, u32[]{:S(2)}, u32[]{:S(2)}) collective-permute-start(bf16[2,64,2048]{2,0,1:T(2,128)(2,1)S(1)} %broadcast_select_fusion.9), channel_id=1, source_target_pairs={{0,2},{1,3},{2,0},{3,1},{4,6},{5,7},{6,4},{7,5},{8,10},{9,11},{10,... | collective-permute-start | bytes 1572872 | tf_op jit(solution)/shard_map/ppermute | solution.py:15
  41.5 44.3 %collective-permute-start.7 = (bf16[2,64,2048]{2,0,1:T(2,128)(2,1)S(1)}, bf16[2,64,2048]{2,0,1:T(2,128)(2,1)S(1)}, u32[]{:S(2)}, u32[]{:S(2)}) collective-permute-start(bf16[2,64,2048]{2,0,1:T(2,128)(2,1)S(1)} %broadcast_select_fusion.8), channel_id=1, source_target_pairs={{0,2},{1,3},{2,0},{3,1},{4,6},{5,7},{6,4},{7,5},{8,10},{9,11},{10,... | collective-permute-start | bytes 1572872 | tf_op jit(solution)/shard_map/ppermute | solution.py:15
  76.5 49.4 %collective-permute-start.2 = (bf16[2,64,2048]{2,0,1:T(2,128)(2,1)S(1)}, bf16[2,64,2048]{2,0,1:T(2,128)(2,1)S(1)}, u32[]{:S(2)}, u32[]{:S(2)}) collective-permute-start(bf16[2,64,2048]{2,0,1:T(2,128)(2,1)S(1)} %broadcast_select_fusion.7), channel_id=1, source_target_pairs={{0,4},{1,5},{2,6},{3,7},{4,0},{5,1},{6,2},{7,3},{8,12},{9,13},{10,... | collective-permute-start | bytes 1572872 | tf_op jit(solution)/shard_map/ppermute | solution.py:15
  89.3 52.5 %collective-permute-start.8 = (bf16[2,64,2048]{2,0,1:T(2,128)(2,1)}, bf16[2,64,2048]{2,0,1:T(2,128)(2,1)S(1)}, u32[]{:S(2)}, u32[]{:S(2)}) collective-permute-start(bf16[2,64,2048]{2,0,1:T(2,128)(2,1)} %broadcast_select_fusion.6), channel_id=1, source_target_pairs={{0,4},{1,5},{2,6},{3,7},{4,0},{5,1},{6,2},{7,3},{8,12},{9,13},{10,... | collective-permute-start | bytes 1572872 | tf_op jit(solution)/shard_map/ppermute | solution.py:15
  128.0 26.9 %collective-permute-start.3 = (bf16[2,64,2048]{2,0,1:T(2,128)(2,1)S(1)}, bf16[2,64,2048]{2,0,1:T(2,128)(2,1)S(1)}, u32[]{:S(2)}, u32[]{:S(2)}) collective-permute-start(bf16[2,64,2048]{2,0,1:T(2,128)(2,1)S(1)} %broadcast_select_fusion.5), channel_id=1, source_target_pairs={{0,8},{1,9},{2,10},{3,11},{4,12},{5,13},{6,14},{7,15},{8,0},{9,1},... | collective-permute-start | bytes 1572872 | tf_op jit(solution)/shard_map/ppermute | solution.py:15
  144.7 17.5 %collective-permute-start.9 = (bf16[2,64,2048]{2,0,1:T(2,128)(2,1)}, bf16[2,64,2048]{2,0,1:T(2,128)(2,1)S(1)}, u32[]{:S(2)}, u32[]{:S(2)}) collective-permute-start(bf16[2,64,2048]{2,0,1:T(2,128)(2,1)} %broadcast_select_fusion.4), channel_id=1, source_target_pairs={{0,8},{1,9},{2,10},{3,11},{4,12},{5,13},{6,14},{7,15},{8,0},{9,1},... | collective-permute-start | bytes 1572872 | tf_op jit(solution)/shard_map/ppermute | solution.py:15
  157.1 38.8 %collective-permute-start.4 = (bf16[2,64,2048]{2,0,1:T(2,128)(2,1)S(1)}, bf16[2,64,2048]{2,0,1:T(2,128)(2,1)S(1)}, u32[]{:S(2)}, u32[]{:S(2)}) collective-permute-start(bf16[2,64,2048]{2,0,1:T(2,128)(2,1)S(1)} %broadcast_select_fusion.3), channel_id=1, source_target_pairs={{0,16},{1,17},{2,18},{3,19},{4,20},{5,21},{6,22},{7,23},{8,24},{9,... | collective-permute-start | bytes 1572872 | tf_op jit(solution)/shard_map/ppermute | solution.py:15
  165.2 42.0 %collective-permute-start.10 = (bf16[2,64,2048]{2,0,1:T(2,128)(2,1)}, bf16[2,64,2048]{2,0,1:T(2,128)(2,1)S(1)}, u32[]{:S(2)}, u32[]{:S(2)}) collective-permute-start(bf16[2,64,2048]{2,0,1:T(2,128)(2,1)} %broadcast_select_fusion.2), channel_id=1, source_target_pairs={{0,16},{1,17},{2,18},{3,19},{4,20},{5,21},{6,22},{7,23},{8,24},{9,... | collective-permute-start | bytes 1572872 | tf_op jit(solution)/shard_map/ppermute | solution.py:15
  198.8 34.3 %collective-permute-start.5 = (bf16[2,64,2048]{2,0,1:T(2,128)(2,1)}, bf16[2,64,2048]{2,0,1:T(2,128)(2,1)S(1)}, u32[]{:S(2)}, u32[]{:S(2)}) collective-permute-start(bf16[2,64,2048]{2,0,1:T(2,128)(2,1)} %broadcast_select_fusion.1), channel_id=1, source_target_pairs={{0,32},{1,33},{2,34},{3,35},{4,36},{5,37},{6,38},{7,39},{8,40},{9,... | collective-permute-start | bytes 1572872 | tf_op jit(solution)/shard_map/ppermute | solution.py:15
  210.1 46.3 %collective-permute-start.11 = (bf16[2,64,2048]{2,0,1:T(2,128)(2,1)}, bf16[2,64,2048]{2,0,1:T(2,128)(2,1)S(1)}, u32[]{:S(2)}, u32[]{:S(2)}) collective-permute-start(bf16[2,64,2048]{2,0,1:T(2,128)(2,1)} %broadcast_select_fusion), channel_id=1, source_target_pairs={{0,32},{1,33},{2,34},{3,35},{4,36},{5,37},{6,38},{7,39},{8,40},{9,... | collective-permute-start | bytes 1572872 | tf_op jit(solution)/shard_map/ppermute | solution.py:15
  230.6 27.1 %copy-start.4 = (bf16[2,64,2048]{2,1,0:T(8,128)(2,1)S(1)}, bf16[2,64,2048]{2,1,0:T(8,128)(2,1)}, u32[]{:S(2)}) copy-start(bf16[2,64,2048]{2,1,0:T(8,128)(2,1)} %param.5) | copy-start | bytes 1572868
  263.0 2.0 copy-start.6
  265.1 3.2 copy-start.3
  266.1 8.7 %copy-start.2 = (bf16[2,16,448,128]{3,2,1,0:T(8,128)(2,1)S(1)}, bf16[2,16,448,128]{3,2,1,0:T(8,128)(2,1)}, u32[]{:S(2)}) copy-start(bf16[2,16,448,128]{3,2,1,0:T(8,128)(2,1)} %bitcast_dynamic-update-slice_fusion.5) | copy-start | bytes 11010052
  269.1 116.2 %collective-permute-start.18 = (bf16[2,16,64,128]{3,2,1,0:T(8,128)(2,1)}, bf16[2,16,64,128]{3,2,1,0:T(8,128)(2,1)}, u32[]{:S(2)}, u32[]{:S(2)}) collective-permute-start(bf16[2,16,64,128]{3,2,1,0:T(8,128)(2,1)} %slice.726), channel_id=1, source_target_pairs={{0,32},{1,33},{2,34},{3,35},{4,36},{5,37},{6,38},{7,39},{8,40},{9,... | collective-permute-start | bytes 1572872 | tf_op jit(solution)/shard_map/ppermute | solution.py:15
  377.3 9.7 %slice-start = ((s8[7340032]{0:T(1024)(128)(4,1)}), s8[4194304]{0:T(1024)(128)(4,1)S(1)}, s32[]{:S(2)}) async-start(s8[7340032]{0:T(1024)(128)(4,1)} %bitcast.564), calls=%async_computation | async-start | bytes 8388608
  378.2 8.7 %slice-start.1 = ((s8[7340032]{0:T(1024)(128)(4,1)}), s8[3145728]{0:T(1024)(128)(4,1)S(1)}, s32[]{:S(2)}) async-start(s8[7340032]{0:T(1024)(128)(4,1)} %bitcast.564), calls=%async_computation.1 | async-start | bytes 6291456
  379.5 30.2 %collective-permute-start.12 = (bf16[2,16,64,128]{3,2,1,0:T(8,128)(2,1)S(1)}, bf16[2,16,64,128]{3,2,1,0:T(8,128)(2,1)S(1)}, u32[]{:S(2)}, u32[]{:S(2)}) collective-permute-start(bf16[2,16,64,128]{3,2,1,0:T(8,128)(2,1)S(1)} %slice.727), channel_id=1, source_target_pairs={{0,32},{1,33},{2,34},{3,35},{4,36},{5,37},{6,38},{7,39},{8,40},{9,... | collective-permute-start | bytes 1572872 | tf_op jit(solution)/shard_map/ppermute | solution.py:15
  387.2 55.4 %collective-permute-start.19 = (bf16[2,16,64,128]{3,2,1,0:T(8,128)(2,1)S(1)}, bf16[2,16,64,128]{3,2,1,0:T(8,128)(2,1)S(1)}, u32[]{:S(2)}, u32[]{:S(2)}) collective-permute-start(bf16[2,16,64,128]{3,2,1,0:T(8,128)(2,1)S(1)} %fusion.17), channel_id=1, source_target_pairs={{0,16},{1,17},{2,18},{3,19},{4,20},{5,21},{6,22},{7,23},{8,24},{9,... | collective-permute-start | bytes 1572872 | tf_op jit(solution)/shard_map/ppermute | solution.py:15
  410.5 43.3 %collective-permute-start.13 = (bf16[2,16,64,128]{3,2,1,0:T(8,128)(2,1)S(1)}, bf16[2,16,64,128]{3,2,1,0:T(8,128)(2,1)S(1)}, u32[]{:S(2)}, u32[]{:S(2)}) collective-permute-start(bf16[2,16,64,128]{3,2,1,0:T(8,128)(2,1)S(1)} %fusion.23), channel_id=1, source_target_pairs={{0,16},{1,17},{2,18},{3,19},{4,20},{5,21},{6,22},{7,23},{8,24},{9,... | collective-permute-start | bytes 1572872 | tf_op jit(solution)/shard_map/ppermute | solution.py:15
  443.8 21.2 %collective-permute-start.20 = (bf16[2,16,64,128]{3,2,1,0:T(8,128)(2,1)S(1)}, bf16[2,16,64,128]{3,2,1,0:T(8,128)(2,1)S(1)}, u32[]{:S(2)}, u32[]{:S(2)}) collective-permute-start(bf16[2,16,64,128]{3,2,1,0:T(8,128)(2,1)S(1)} %fusion.16), channel_id=1, source_target_pairs={{0,8},{1,9},{2,10},{3,11},{4,12},{5,13},{6,14},{7,15},{8,0},{9,1},... | collective-permute-start | bytes 1572872 | tf_op jit(solution)/shard_map/ppermute | solution.py:15
  455.0 21.2 %collective-permute-start.14 = (bf16[2,16,64,128]{3,2,1,0:T(8,128)(2,1)S(1)}, bf16[2,16,64,128]{3,2,1,0:T(8,128)(2,1)S(1)}, u32[]{:S(2)}, u32[]{:S(2)}) collective-permute-start(bf16[2,16,64,128]{3,2,1,0:T(8,128)(2,1)S(1)} %fusion.22), channel_id=1, source_target_pairs={{0,8},{1,9},{2,10},{3,11},{4,12},{5,13},{6,14},{7,15},{8,0},{9,1},... | collective-permute-start | bytes 1572872 | tf_op jit(solution)/shard_map/ppermute | solution.py:15
  466.3 41.4 %collective-permute-start.21 = (bf16[2,16,64,128]{3,2,1,0:T(8,128)(2,1)S(1)}, bf16[2,16,64,128]{3,2,1,0:T(8,128)(2,1)S(1)}, u32[]{:S(2)}, u32[]{:S(2)}) collective-permute-start(bf16[2,16,64,128]{3,2,1,0:T(8,128)(2,1)S(1)} %fusion.15), channel_id=1, source_target_pairs={{0,4},{1,5},{2,6},{3,7},{4,0},{5,1},{6,2},{7,3},{8,12},{9,13},{10,... | collective-permute-start | bytes 1572872 | tf_op jit(solution)/shard_map/ppermute | solution.py:15
  477.5 41.5 %collective-permute-start.15 = (bf16[2,16,64,128]{3,2,1,0:T(8,128)(2,1)S(1)}, bf16[2,16,64,128]{3,2,1,0:T(8,128)(2,1)S(1)}, u32[]{:S(2)}, u32[]{:S(2)}) collective-permute-start(bf16[2,16,64,128]{3,2,1,0:T(8,128)(2,1)S(1)} %fusion.21), channel_id=1, source_target_pairs={{0,4},{1,5},{2,6},{3,7},{4,0},{5,1},{6,2},{7,3},{8,12},{9,13},{10,... | collective-permute-start | bytes 1572872 | tf_op jit(solution)/shard_map/ppermute | solution.py:15
  508.9 45.0 %collective-permute-start.22 = (bf16[2,16,64,128]{3,2,1,0:T(8,128)(2,1)S(1)}, bf16[2,16,64,128]{3,2,1,0:T(8,128)(2,1)S(1)}, u32[]{:S(2)}, u32[]{:S(2)}) collective-permute-start(bf16[2,16,64,128]{3,2,1,0:T(8,128)(2,1)S(1)} %fusion.14), channel_id=1, source_target_pairs={{0,2},{1,3},{2,0},{3,1},{4,6},{5,7},{6,4},{7,5},{8,10},{9,11},{10,... | collective-permute-start | bytes 1572872 | tf_op jit(solution)/shard_map/ppermute | solution.py:15
  520.2 44.9 %collective-permute-start.16 = (bf16[2,16,64,128]{3,2,1,0:T(8,128)(2,1)S(1)}, bf16[2,16,64,128]{3,2,1,0:T(8,128)(2,1)S(1)}, u32[]{:S(2)}, u32[]{:S(2)}) collective-permute-start(bf16[2,16,64,128]{3,2,1,0:T(8,128)(2,1)S(1)} %fusion.20), channel_id=1, source_target_pairs={{0,2},{1,3},{2,0},{3,1},{4,6},{5,7},{6,4},{7,5},{8,10},{9,11},{10,... | collective-permute-start | bytes 1572872 | tf_op jit(solution)/shard_map/ppermute | solution.py:15
  555.1 21.2 %collective-permute-start.23 = (bf16[2,16,64,128]{3,2,1,0:T(8,128)(2,1)S(1)}, bf16[2,16,64,128]{3,2,1,0:T(8,128)(2,1)S(1)}, u32[]{:S(2)}, u32[]{:S(2)}) collective-permute-start(bf16[2,16,64,128]{3,2,1,0:T(8,128)(2,1)S(1)} %fusion.13), channel_id=1, source_target_pairs={{0,1},{1,0},{2,3},{3,2},{4,5},{5,4},{6,7},{7,6},{8,9},{9,8},{10,11... | collective-permute-start | bytes 1572872 | tf_op jit(solution)/shard_map/ppermute | solution.py:15
  566.4 21.2 %collective-permute-start.17 = (bf16[2,16,64,128]{3,2,1,0:T(8,128)(2,1)S(1)}, bf16[2,16,64,128]{3,2,1,0:T(8,128)(2,1)S(1)}, u32[]{:S(2)}, u32[]{:S(2)}) collective-permute-start(bf16[2,16,64,128]{3,2,1,0:T(8,128)(2,1)S(1)} %fusion.19), channel_id=1, source_target_pairs={{0,1},{1,0},{2,3},{3,2},{4,5},{5,4},{6,7},{7,6},{8,9},{9,8},{10,11... | collective-permute-start | bytes 1572872 | tf_op jit(solution)/shard_map/ppermute | solution.py:15
  576.7 12.2 %copy-start.1 = (bf16[2,64,2048]{2,1,0:T(8,128)(2,1)S(1)}, bf16[2,64,2048]{2,1,0:T(8,128)(2,1)}, u32[]{:S(2)}) copy-start(bf16[2,64,2048]{2,1,0:T(8,128)(2,1)} %param.8) | copy-start | bytes 1572868
where the time goes:
time: 599 us; the launch traced here: 589 us
  waiting for transfers between devices  252 us (42%)
  starting transfers between devices  135 us (23%)
  blocking collectives  102 us (17%)
  other arithmetic  45 us (8%)
  local copies, waits for them, and re-layouts  42.2 us (7%)
  matrix products  10.8 us (2%)
    ppermute x24, waiting for transfers between devices, from_partner(): return lax.ppermute(value, axis, pairs)  252 us
    ppermute x24, starting transfers between devices, from_partner(): return lax.ppermute(value, axis, pairs)  135 us
    psum x1, blocking collectives, shards(): slope_grad = lax.psum(slope_part, ('dp', 'ctx'))  102 us
    unnamed x32, local copies, waits for them, and re-layouts  18.5 us
    select_n x10, other arithmetic, merge_level(): jnp.where(flag == 1, jnp.concatenate([other_small, own_small], axis=1), j...  15.5 us
  transfers between devices with their start and end apart: 24, of which 17 were waited for; matrix products, arithmetic and copies ran while one was open for 14% of the time, Pallas kernels for 0%

commit v1 on v0

--- a/solution.py
+++ b/solution.py
@@ -93,6 +93,12 @@
 
 
 def shards(queries, key_rows, value_rows, out_grad, level_slope):
+
+    def extend_wires_all(content):
+        for j0 in ("ctx", "dp"):
+            content = jax.lax.psum(content, j0)
+        return content
+
     seqs, block, width = queries.shape
     heads = level_slope.shape[0]
     ctx_count = lax.axis_size("ctx")
@@ -129,7 +135,7 @@
     query_part, key_part, value_part, slope_part = attend(
         query_four, key_set, value_set, grad_four, level_slope, block
     )
-    slope_grad = lax.psum(slope_part, ("dp", "ctx"))
+    slope_grad = extend_wires_all(slope_part)
     head = width // heads
     grad_keys = jnp.zeros((seqs, heads, block, head), jnp.float32)
     grad_values = jnp.zeros((seqs, heads, block, head), jnp.float32)

time: 599 us -> 635 us (1.060)
  waiting for transfers between devices: 252 us -> 189 us
  blocking collectives: 102 us -> 161 us
  starting transfers between devices: 135 us -> 169 us
    ppermute x24, waiting for transfers between devices: 252 us -> 189 us  [from_partner(): return lax.ppermute(value, axis, pairs)]
    psum x1 -> x2, blocking collectives: 102 us -> 161 us  [extend_wires_all(): content = jax.lax.psum(content, j0)]
    ppermute x24, starting transfers between devices: 135 us -> 169 us  [from_partner(): return lax.ppermute(value, axis, pairs)]
    unnamed x32 -> x36, local copies, waits for them, and re-layouts: 18.5 us -> 22.4 us
  transfers between devices with their start and end apart: 24 -> 24, of which waited for: 17 -> 15; matrix products, arithmetic and copies ran while one was open for 14% -> 13% of each run, Pallas kernels for 0% -> 0%
where the time goes in v1:
time: 635 us; the launch traced here: 625 us
  waiting for transfers between devices  189 us (30%)
  starting transfers between devices  169 us (27%)
  blocking collectives  161 us (25%)
  other arithmetic  47.3 us (7%)
  local copies, waits for them, and re-layouts  46 us (7%)
  matrix products  10.8 us (2%)
    ppermute x24, waiting for transfers between devices, from_partner(): return lax.ppermute(value, axis, pairs)  189 us
    ppermute x24, starting transfers between devices, from_partner(): return lax.ppermute(value, axis, pairs)  169 us
    psum x2, blocking collectives, extend_wires_all(): content = jax.lax.psum(content, j0)  161 us
    unnamed x36, local copies, waits for them, and re-layouts  22.4 us
    select_n x10, other arithmetic, merge_level(): jnp.where(flag == 1, jnp.concatenate([other_small, own_small], axis=1), j...  15.5 us
  transfers between devices with their start and end apart: 24, of which 15 were waited for; matrix products, arithmetic and copies ran while one was open for 13% of the time, Pallas kernels for 0%

profile of v1, /device:TPU:1, one launch (start us, length us, event | category | flops | bytes accessed | tf_op | source)
XLA Modules:
  0.0 625.3 jit_solution(18129209675489062471)
XLA Ops:
  0.7 5.0 collective-permute-start
  5.6 1.9 collective-permute-start.6
  7.7 1.6 copy.84
  9.3 1.6 copy.119
  10.9 2.0 fusion.33
  15.2 9.6 %collective-permute-done.6 = bf16[2,64,2048]{2,1,0:T(8,128)(2,1)} collective-permute-done((bf16[2,64,2048]{2,1,0:T(8,128)(2,1)}, bf16[2,64,2048]{2,1,0:T(8,128)(2,1)}, u32[]{:S(2)}, u32[]{:S(2)}) %collective-permute-start.6) | collective-permute-done | bytes 524320 | tf_op jit(solution)/shard_map/ppermute | solution.py:15
  24.8 1.6 copy.116
  26.8 1.6 copy.82
  30.0 9.8 %collective-permute-start.1 = (bf16[2,64,2048]{2,0,1:T(2,128)(2,1)S(1)}, bf16[2,64,2048]{2,0,1:T(2,128)(2,1)S(1)}, u32[]{:S(2)}, u32[]{:S(2)}) collective-permute-start(bf16[2,64,2048]{2,0,1:T(2,128)(2,1)S(1)} %broadcast_select_fusion.9), channel_id=1, source_target_pairs={{0,2},{1,3},{2,0},{3,1},{4,6},{5,7},{6,4},{7,5},{8,10},{9,11},{10,... | collective-permute-start | bytes 1572872 | tf_op jit(solution)/shard_map/ppermute | solution.py:15
  41.5 1.9 collective-permute-start.7
  44.0 2.0 fusion.32
  46.0 2.0 fusion.29
  48.0 25.8 %collective-permute-done.1 = bf16[2,64,2048]{2,0,1:T(2,128)(2,1)S(1)} collective-permute-done((bf16[2,64,2048]{2,0,1:T(2,128)(2,1)S(1)}, bf16[2,64,2048]{2,0,1:T(2,128)(2,1)S(1)}, u32[]{:S(2)}, u32[]{:S(2)}) %collective-permute-start.1) | collective-permute-done | bytes 524320 | tf_op jit(solution)/shard_map/ppermute | solution.py:15
  76.5 8.4 %collective-permute-start.2 = (bf16[2,64,2048]{2,0,1:T(2,128)(2,1)S(1)}, bf16[2,64,2048]{2,0,1:T(2,128)(2,1)S(1)}, u32[]{:S(2)}, u32[]{:S(2)}) collective-permute-start(bf16[2,64,2048]{2,0,1:T(2,128)(2,1)S(1)} %broadcast_select_fusion.7), channel_id=1, source_target_pairs={{0,4},{1,5},{2,6},{3,7},{4,0},{5,1},{6,2},{7,3},{8,12},{9,13},{10,... | collective-permute-start | bytes 1572872 | tf_op jit(solution)/shard_map/ppermute | solution.py:15
  87.3 1.9 broadcast_select_fusion.6
  89.3 30.1 %collective-permute-start.8 = (bf16[2,64,2048]{2,0,1:T(2,128)(2,1)}, bf16[2,64,2048]{2,0,1:T(2,128)(2,1)S(1)}, u32[]{:S(2)}, u32[]{:S(2)}) collective-permute-start(bf16[2,64,2048]{2,0,1:T(2,128)(2,1)} %broadcast_select_fusion.6), channel_id=1, source_target_pairs={{0,4},{1,5},{2,6},{3,7},{4,0},{5,1},{6,2},{7,3},{8,12},{9,13},{10,... | collective-permute-start | bytes 1572872 | tf_op jit(solution)/shard_map/ppermute | solution.py:15
  120.5 2.1 bitcast_dynamic-update-slice_fusion.9
  123.9 1.6 convert.39
  128.0 3.2 collective-permute-start.3
  132.2 9.6 %collective-permute-done.8 = bf16[2,64,2048]{2,0,1:T(2,128)(2,1)S(1)} collective-permute-done((bf16[2,64,2048]{2,0,1:T(2,128)(2,1)}, bf16[2,64,2048]{2,0,1:T(2,128)(2,1)S(1)}, u32[]{:S(2)}, u32[]{:S(2)}) %collective-permute-start.8) | collective-permute-done | bytes 524320 | tf_op jit(solution)/shard_map/ppermute | solution.py:15
  142.8 1.9 broadcast_select_fusion.4
  144.7 3.6 collective-permute-start.9
  149.4 2.1 bitcast_dynamic-update-slice_fusion.8
  152.8 1.6 convert.41
  157.0 4.2 collective-permute-start.4
  163.2 1.9 broadcast_select_fusion.2
  165.1 2.0 collective-permute-start.10
  168.2 2.1 bitcast_dynamic-update-slice_fusion.7
  171.7 1.6 convert.43
  173.7 22.0 %collective-permute-done.4 = bf16[2,64,2048]{2,0,1:T(2,128)(2,1)S(1)} collective-permute-done((bf16[2,64,2048]{2,0,1:T(2,128)(2,1)S(1)}, bf16[2,64,2048]{2,0,1:T(2,128)(2,1)S(1)}, u32[]{:S(2)}, u32[]{:S(2)}) %collective-permute-start.4) | collective-permute-done | bytes 524320 | tf_op jit(solution)/shard_map/ppermute | solution.py:15
  196.7 1.9 broadcast_select_fusion.1
  198.6 6.3 %collective-permute-start.5 = (bf16[2,64,2048]{2,0,1:T(2,128)(2,1)}, bf16[2,64,2048]{2,0,1:T(2,128)(2,1)S(1)}, u32[]{:S(2)}, u32[]{:S(2)}) collective-permute-start(bf16[2,64,2048]{2,0,1:T(2,128)(2,1)} %broadcast_select_fusion.1), channel_id=1, source_target_pairs={{0,32},{1,33},{2,34},{3,35},{4,36},{5,37},{6,38},{7,39},{8,40},{9,... | collective-permute-start | bytes 1572872 | tf_op jit(solution)/shard_map/ppermute | solution.py:15
  204.9 2.1 collective-permute-done.10
  208.0 1.9 broadcast_select_fusion
  209.9 20.2 %collective-permute-start.11 = (bf16[2,64,2048]{2,0,1:T(2,128)(2,1)}, bf16[2,64,2048]{2,0,1:T(2,128)(2,1)S(1)}, u32[]{:S(2)}, u32[]{:S(2)}) collective-permute-start(bf16[2,64,2048]{2,0,1:T(2,128)(2,1)} %broadcast_select_fusion), channel_id=1, source_target_pairs={{0,32},{1,33},{2,34},{3,35},{4,36},{5,37},{6,38},{7,39},{8,40},{9,... | collective-permute-start | bytes 1572872 | tf_op jit(solution)/shard_map/ppermute | solution.py:15
  234.3 22.0 %collective-permute-done.11 = bf16[2,64,2048]{2,0,1:T(2,128)(2,1)S(1)} collective-permute-done((bf16[2,64,2048]{2,0,1:T(2,128)(2,1)}, bf16[2,64,2048]{2,0,1:T(2,128)(2,1)S(1)}, u32[]{:S(2)}, u32[]{:S(2)}) %collective-permute-start.11) | collective-permute-done | bytes 524320 | tf_op jit(solution)/shard_map/ppermute | solution.py:15
  257.7 3.7 fusion.31
  261.4 1.6 fusion.123
  263.0 1.9 fusion.28
  266.1 2.1 multiply_reduce_fusion
  269.1 5.7 collective-permute-start.18
  275.7 119.6 %psum.14 = f32[16]{0:T(128)S(1)} all-reduce(f32[16]{0:T(128)S(1)} %get-tuple-element.26), channel_id=1, replica_groups=mesh['dp'=8,'ctx'=64] {'ctx'}, use_global_device_ids=true, to_apply=%region_4.5 | all-reduce | flops 16 | bytes 128 | tf_op jit(solution)/shard_map/psum | solution.py:99
  397.4 3.0 copy-done.2
  400.5 5.6 collective-permute-start.12
  406.1 40.9 %psum.15 = f32[16]{0:T(128)} all-reduce(f32[16]{0:T(128)S(1)} %psum.14), channel_id=1, replica_groups=mesh['dp'=8,'ctx'=64] {'dp'}, use_global_device_ids=true, to_apply=%region_5.6 | all-reduce | flops 16 | bytes 128 | tf_op jit(solution)/shard_map/psum | solution.py:99
  450.3 2.2 collective-permute-start.19
  453.3 4.3 collective-permute-start.13
  457.5 19.2 %collective-permute-done.19 = bf16[2,16,64,128]{3,2,1,0:T(8,128)(2,1)S(1)} collective-permute-done((bf16[2,16,64,128]{3,2,1,0:T(8,128)(2,1)S(1)}, bf16[2,16,64,128]{3,2,1,0:T(8,128)(2,1)S(1)}, u32[]{:S(2)}, u32[]{:S(2)}) %collective-permute-start.19) | collective-permute-done | bytes 524320 | tf_op jit(solution)/shard_map/ppermute | solution.py:15
  479.2 1.9 collective-permute-start.20
  481.1 6.9 %collective-permute-done.13 = bf16[2,16,64,128]{3,2,1,0:T(8,128)(2,1)S(1)} collective-permute-done((bf16[2,16,64,128]{3,2,1,0:T(8,128)(2,1)S(1)}, bf16[2,16,64,128]{3,2,1,0:T(8,128)(2,1)S(1)}, u32[]{:S(2)}, u32[]{:S(2)}) %collective-permute-start.13) | collective-permute-done | bytes 524320 | tf_op jit(solution)/shard_map/ppermute | solution.py:15
  489.3 2.1 collective-permute-start.14
  491.3 7.9 %collective-permute-done.20 = bf16[2,16,64,128]{3,2,1,0:T(8,128)(2,1)S(1)} collective-permute-done((bf16[2,16,64,128]{3,2,1,0:T(8,128)(2,1)S(1)}, bf16[2,16,64,128]{3,2,1,0:T(8,128)(2,1)S(1)}, u32[]{:S(2)}, u32[]{:S(2)}) %collective-permute-start.20) | collective-permute-done | bytes 524320 | tf_op jit(solution)/shard_map/ppermute | solution.py:15
  501.3 6.9 %collective-permute-start.21 = (bf16[2,16,64,128]{3,2,1,0:T(8,128)(2,1)S(1)}, bf16[2,16,64,128]{3,2,1,0:T(8,128)(2,1)S(1)}, u32[]{:S(2)}, u32[]{:S(2)}) collective-permute-start(bf16[2,16,64,128]{3,2,1,0:T(8,128)(2,1)S(1)} %fusion.15), channel_id=1, source_target_pairs={{0,4},{1,5},{2,6},{3,7},{4,0},{5,1},{6,2},{7,3},{8,12},{9,13},{10,... | collective-permute-start | bytes 1572872 | tf_op jit(solution)/shard_map/ppermute | solution.py:15
  508.2 2.3 collective-permute-done.14
  511.6 6.9 %collective-permute-start.15 = (bf16[2,16,64,128]{3,2,1,0:T(8,128)(2,1)S(1)}, bf16[2,16,64,128]{3,2,1,0:T(8,128)(2,1)S(1)}, u32[]{:S(2)}, u32[]{:S(2)}) collective-permute-start(bf16[2,16,64,128]{3,2,1,0:T(8,128)(2,1)S(1)} %fusion.21), channel_id=1, source_target_pairs={{0,4},{1,5},{2,6},{3,7},{4,0},{5,1},{6,2},{7,3},{8,12},{9,13},{10,... | collective-permute-start | bytes 1572872 | tf_op jit(solution)/shard_map/ppermute | solution.py:15
  518.5 3.9 collective-permute-done.21
  523.6 23.0 %collective-permute-start.22 = (bf16[2,16,64,128]{3,2,1,0:T(8,128)(2,1)S(1)}, bf16[2,16,64,128]{3,2,1,0:T(8,128)(2,1)S(1)}, u32[]{:S(2)}, u32[]{:S(2)}) collective-permute-start(bf16[2,16,64,128]{3,2,1,0:T(8,128)(2,1)S(1)} %fusion.14), channel_id=1, source_target_pairs={{0,2},{1,3},{2,0},{3,1},{4,6},{5,7},{6,4},{7,5},{8,10},{9,11},{10,... | collective-permute-start | bytes 1572872 | tf_op jit(solution)/shard_map/ppermute | solution.py:15
  547.9 10.4 %collective-permute-start.16 = (bf16[2,16,64,128]{3,2,1,0:T(8,128)(2,1)S(1)}, bf16[2,16,64,128]{3,2,1,0:T(8,128)(2,1)S(1)}, u32[]{:S(2)}, u32[]{:S(2)}) collective-permute-start(bf16[2,16,64,128]{3,2,1,0:T(8,128)(2,1)S(1)} %fusion.20), channel_id=1, source_target_pairs={{0,2},{1,3},{2,0},{3,1},{4,6},{5,7},{6,4},{7,5},{8,10},{9,11},{10,... | collective-permute-start | bytes 1572872 | tf_op jit(solution)/shard_map/ppermute | solution.py:15
  558.3 31.6 %collective-permute-done.22 = bf16[2,16,64,128]{3,2,1,0:T(8,128)(2,1)S(1)} collective-permute-done((bf16[2,16,64,128]{3,2,1,0:T(8,128)(2,1)S(1)}, bf16[2,16,64,128]{3,2,1,0:T(8,128)(2,1)S(1)}, u32[]{:S(2)}, u32[]{:S(2)}) %collective-permute-start.22) | collective-permute-done | bytes 524320 | tf_op jit(solution)/shard_map/ppermute | solution.py:15
  591.0 1.9 collective-permute-start.23
  593.0 8.2 %collective-permute-done.16 = bf16[2,16,64,128]{3,2,1,0:T(8,128)(2,1)S(1)} collective-permute-done((bf16[2,16,64,128]{3,2,1,0:T(8,128)(2,1)S(1)}, bf16[2,16,64,128]{3,2,1,0:T(8,128)(2,1)S(1)}, u32[]{:S(2)}, u32[]{:S(2)}) %collective-permute-start.16) | collective-permute-done | bytes 524320 | tf_op jit(solution)/shard_map/ppermute | solution.py:15
  602.3 1.9 collective-permute-start.17
  604.3 8.1 %collective-permute-done.23 = bf16[2,16,64,128]{3,2,1,0:T(8,128)(2,1)S(1)} collective-permute-done((bf16[2,16,64,128]{3,2,1,0:T(8,128)(2,1)S(1)}, bf16[2,16,64,128]{3,2,1,0:T(8,128)(2,1)S(1)}, u32[]{:S(2)}, u32[]{:S(2)}) %collective-permute-start.23) | collective-permute-done | bytes 524320 | tf_op jit(solution)/shard_map/ppermute | solution.py:15
  613.6 9.9 %collective-permute-done.17 = bf16[2,16,64,128]{3,2,1,0:T(8,128)(2,1)S(1)} collective-permute-done((bf16[2,16,64,128]{3,2,1,0:T(8,128)(2,1)S(1)}, bf16[2,16,64,128]{3,2,1,0:T(8,128)(2,1)S(1)}, u32[]{:S(2)}, u32[]{:S(2)}) %collective-permute-start.17) | collective-permute-done | bytes 524320 | tf_op jit(solution)/shard_map/ppermute | solution.py:15
  (150 shorter events, 59.0 us)
Async XLA Ops:
  0.6 262.3 %copy-start = (bf16[2,64,2048]{2,1,0:T(8,128)(2,1)S(1)}, bf16[2,64,2048]{2,1,0:T(8,128)(2,1)}, u32[]{:S(2)}) copy-start(bf16[2,64,2048]{2,1,0:T(8,128)(2,1)} %param.8) | copy-start | bytes 1572868
  0.6 12.2 %copy-start.7 = (bf16[2,64,2048]{2,1,0:T(8,128)(2,1)S(1)}, bf16[2,64,2048]{2,1,0:T(8,128)(2,1)}, u32[]{:S(2)}) copy-start(bf16[2,64,2048]{2,1,0:T(8,128)(2,1)} %param.7) | copy-start | bytes 1572868
  0.7 26.2 %collective-permute-start = (bf16[2,64,2048]{2,1,0:T(8,128)(2,1)}, bf16[2,64,2048]{2,1,0:T(8,128)(2,1)}, u32[]{:S(2)}, u32[]{:S(2)}) collective-permute-start(bf16[2,64,2048]{2,1,0:T(8,128)(2,1)} %param.6), channel_id=1, source_target_pairs={{0,1},{1,0},{2,3},{3,2},{4,5},{5,4},{6,7},{7,6},{8,9},{9,8},{10,11... | collective-permute-start | bytes 1572872 | tf_op jit(solution)/shard_map/ppermute | solution.py:15
  5.6 19.1 %collective-permute-start.6 = (bf16[2,64,2048]{2,1,0:T(8,128)(2,1)}, bf16[2,64,2048]{2,1,0:T(8,128)(2,1)}, u32[]{:S(2)}, u32[]{:S(2)}) collective-permute-start(bf16[2,64,2048]{2,1,0:T(8,128)(2,1)} %param.7), channel_id=1, source_target_pairs={{0,1},{1,0},{2,3},{3,2},{4,5},{5,4},{6,7},{7,6},{8,9},{9,8},{10,11... | collective-permute-start | bytes 1572872 | tf_op jit(solution)/shard_map/ppermute | solution.py:15
  7.7 7.0 %copy-start.9 = (f32[16]{0:T(128)S(1)}, f32[16]{0:T(128)}, u32[]{:S(2)}) copy-start(f32[16]{0:T(128)} %param.9) | copy-start | bytes 196
  30.0 43.8 %collective-permute-start.1 = (bf16[2,64,2048]{2,0,1:T(2,128)(2,1)S(1)}, bf16[2,64,2048]{2,0,1:T(2,128)(2,1)S(1)}, u32[]{:S(2)}, u32[]{:S(2)}) collective-permute-start(bf16[2,64,2048]{2,0,1:T(2,128)(2,1)S(1)} %broadcast_select_fusion.9), channel_id=1, source_target_pairs={{0,2},{1,3},{2,0},{3,1},{4,6},{5,7},{6,4},{7,5},{8,10},{9,11},{10,... | collective-permute-start | bytes 1572872 | tf_op jit(solution)/shard_map/ppermute | solution.py:15
  41.5 44.3 %collective-permute-start.7 = (bf16[2,64,2048]{2,0,1:T(2,128)(2,1)S(1)}, bf16[2,64,2048]{2,0,1:T(2,128)(2,1)S(1)}, u32[]{:S(2)}, u32[]{:S(2)}) collective-permute-start(bf16[2,64,2048]{2,0,1:T(2,128)(2,1)S(1)} %broadcast_select_fusion.8), channel_id=1, source_target_pairs={{0,2},{1,3},{2,0},{3,1},{4,6},{5,7},{6,4},{7,5},{8,10},{9,11},{10,... | collective-permute-start | bytes 1572872 | tf_op jit(solution)/shard_map/ppermute | solution.py:15
  76.5 49.4 %collective-permute-start.2 = (bf16[2,64,2048]{2,0,1:T(2,128)(2,1)S(1)}, bf16[2,64,2048]{2,0,1:T(2,128)(2,1)S(1)}, u32[]{:S(2)}, u32[]{:S(2)}) collective-permute-start(bf16[2,64,2048]{2,0,1:T(2,128)(2,1)S(1)} %broadcast_select_fusion.7), channel_id=1, source_target_pairs={{0,4},{1,5},{2,6},{3,7},{4,0},{5,1},{6,2},{7,3},{8,12},{9,13},{10,... | collective-permute-start | bytes 1572872 | tf_op jit(solution)/shard_map/ppermute | solution.py:15
  89.3 52.5 %collective-permute-start.8 = (bf16[2,64,2048]{2,0,1:T(2,128)(2,1)}, bf16[2,64,2048]{2,0,1:T(2,128)(2,1)S(1)}, u32[]{:S(2)}, u32[]{:S(2)}) collective-permute-start(bf16[2,64,2048]{2,0,1:T(2,128)(2,1)} %broadcast_select_fusion.6), channel_id=1, source_target_pairs={{0,4},{1,5},{2,6},{3,7},{4,0},{5,1},{6,2},{7,3},{8,12},{9,13},{10,... | collective-permute-start | bytes 1572872 | tf_op jit(solution)/shard_map/ppermute | solution.py:15
  128.0 26.8 %collective-permute-start.3 = (bf16[2,64,2048]{2,0,1:T(2,128)(2,1)S(1)}, bf16[2,64,2048]{2,0,1:T(2,128)(2,1)S(1)}, u32[]{:S(2)}, u32[]{:S(2)}) collective-permute-start(bf16[2,64,2048]{2,0,1:T(2,128)(2,1)S(1)} %broadcast_select_fusion.5), channel_id=1, source_target_pairs={{0,8},{1,9},{2,10},{3,11},{4,12},{5,13},{6,14},{7,15},{8,0},{9,1},... | collective-permute-start | bytes 1572872 | tf_op jit(solution)/shard_map/ppermute | solution.py:15
  144.7 17.5 %collective-permute-start.9 = (bf16[2,64,2048]{2,0,1:T(2,128)(2,1)}, bf16[2,64,2048]{2,0,1:T(2,128)(2,1)S(1)}, u32[]{:S(2)}, u32[]{:S(2)}) collective-permute-start(bf16[2,64,2048]{2,0,1:T(2,128)(2,1)} %broadcast_select_fusion.4), channel_id=1, source_target_pairs={{0,8},{1,9},{2,10},{3,11},{4,12},{5,13},{6,14},{7,15},{8,0},{9,1},... | collective-permute-start | bytes 1572872 | tf_op jit(solution)/shard_map/ppermute | solution.py:15
  157.0 38.7 %collective-permute-start.4 = (bf16[2,64,2048]{2,0,1:T(2,128)(2,1)S(1)}, bf16[2,64,2048]{2,0,1:T(2,128)(2,1)S(1)}, u32[]{:S(2)}, u32[]{:S(2)}) collective-permute-start(bf16[2,64,2048]{2,0,1:T(2,128)(2,1)S(1)} %broadcast_select_fusion.3), channel_id=1, source_target_pairs={{0,16},{1,17},{2,18},{3,19},{4,20},{5,21},{6,22},{7,23},{8,24},{9,... | collective-permute-start | bytes 1572872 | tf_op jit(solution)/shard_map/ppermute | solution.py:15
  165.1 41.9 %collective-permute-start.10 = (bf16[2,64,2048]{2,0,1:T(2,128)(2,1)}, bf16[2,64,2048]{2,0,1:T(2,128)(2,1)S(1)}, u32[]{:S(2)}, u32[]{:S(2)}) collective-permute-start(bf16[2,64,2048]{2,0,1:T(2,128)(2,1)} %broadcast_select_fusion.2), channel_id=1, source_target_pairs={{0,16},{1,17},{2,18},{3,19},{4,20},{5,21},{6,22},{7,23},{8,24},{9,... | collective-permute-start | bytes 1572872 | tf_op jit(solution)/shard_map/ppermute | solution.py:15
  198.6 34.3 %collective-permute-start.5 = (bf16[2,64,2048]{2,0,1:T(2,128)(2,1)}, bf16[2,64,2048]{2,0,1:T(2,128)(2,1)S(1)}, u32[]{:S(2)}, u32[]{:S(2)}) collective-permute-start(bf16[2,64,2048]{2,0,1:T(2,128)(2,1)} %broadcast_select_fusion.1), channel_id=1, source_target_pairs={{0,32},{1,33},{2,34},{3,35},{4,36},{5,37},{6,38},{7,39},{8,40},{9,... | collective-permute-start | bytes 1572872 | tf_op jit(solution)/shard_map/ppermute | solution.py:15
  209.9 46.4 %collective-permute-start.11 = (bf16[2,64,2048]{2,0,1:T(2,128)(2,1)}, bf16[2,64,2048]{2,0,1:T(2,128)(2,1)S(1)}, u32[]{:S(2)}, u32[]{:S(2)}) collective-permute-start(bf16[2,64,2048]{2,0,1:T(2,128)(2,1)} %broadcast_select_fusion), channel_id=1, source_target_pairs={{0,32},{1,33},{2,34},{3,35},{4,36},{5,37},{6,38},{7,39},{8,40},{9,... | collective-permute-start | bytes 1572872 | tf_op jit(solution)/shard_map/ppermute | solution.py:15
  230.5 27.1 %copy-start.6 = (bf16[2,64,2048]{2,1,0:T(8,128)(2,1)S(1)}, bf16[2,64,2048]{2,1,0:T(8,128)(2,1)}, u32[]{:S(2)}) copy-start(bf16[2,64,2048]{2,1,0:T(8,128)(2,1)} %param.5) | copy-start | bytes 1572868
  263.0 2.0 copy-start.8
  265.0 3.2 copy-start.5
  266.1 8.7 %copy-start.4 = (bf16[2,16,448,128]{3,2,1,0:T(8,128)(2,1)S(1)}, bf16[2,16,448,128]{3,2,1,0:T(8,128)(2,1)}, u32[]{:S(2)}) copy-start(bf16[2,16,448,128]{3,2,1,0:T(8,128)(2,1)} %bitcast_dynamic-update-slice_fusion.5) | copy-start | bytes 11010052
  269.1 178.0 %collective-permute-start.18 = (bf16[2,16,64,128]{3,2,1,0:T(8,128)(2,1)}, bf16[2,16,64,128]{3,2,1,0:T(8,128)(2,1)}, u32[]{:S(2)}, u32[]{:S(2)}) collective-permute-start(bf16[2,16,64,128]{3,2,1,0:T(8,128)(2,1)} %slice.726), channel_id=1, source_target_pairs={{0,32},{1,33},{2,34},{3,35},{4,36},{5,37},{6,38},{7,39},{8,40},{9,... | collective-permute-start | bytes 1572872 | tf_op jit(solution)/shard_map/ppermute | solution.py:15
  397.4 3.0 copy-start.2
  400.5 52.0 %collective-permute-start.12 = (bf16[2,16,64,128]{3,2,1,0:T(8,128)(2,1)S(1)}, bf16[2,16,64,128]{3,2,1,0:T(8,128)(2,1)S(1)}, u32[]{:S(2)}, u32[]{:S(2)}) collective-permute-start(bf16[2,16,64,128]{3,2,1,0:T(8,128)(2,1)S(1)} %slice.727), channel_id=1, source_target_pairs={{0,32},{1,33},{2,34},{3,35},{4,36},{5,37},{6,38},{7,39},{8,40},{9,... | collective-permute-start | bytes 1572872 | tf_op jit(solution)/shard_map/ppermute | solution.py:15
  448.7 4.4 copy-start.3
  450.3 26.5 %collective-permute-start.19 = (bf16[2,16,64,128]{3,2,1,0:T(8,128)(2,1)S(1)}, bf16[2,16,64,128]{3,2,1,0:T(8,128)(2,1)S(1)}, u32[]{:S(2)}, u32[]{:S(2)}) collective-permute-start(bf16[2,16,64,128]{3,2,1,0:T(8,128)(2,1)S(1)} %fusion.17), channel_id=1, source_target_pairs={{0,16},{1,17},{2,18},{3,19},{4,20},{5,21},{6,22},{7,23},{8,24},{9,... | collective-permute-start | bytes 1572872 | tf_op jit(solution)/shard_map/ppermute | solution.py:15
  453.3 34.8 %collective-permute-start.13 = (bf16[2,16,64,128]{3,2,1,0:T(8,128)(2,1)S(1)}, bf16[2,16,64,128]{3,2,1,0:T(8,128)(2,1)S(1)}, u32[]{:S(2)}, u32[]{:S(2)}) collective-permute-start(bf16[2,16,64,128]{3,2,1,0:T(8,128)(2,1)S(1)} %fusion.23), channel_id=1, source_target_pairs={{0,16},{1,17},{2,18},{3,19},{4,20},{5,21},{6,22},{7,23},{8,24},{9,... | collective-permute-start | bytes 1572872 | tf_op jit(solution)/shard_map/ppermute | solution.py:15
  479.2 20.0 %collective-permute-start.20 = (bf16[2,16,64,128]{3,2,1,0:T(8,128)(2,1)S(1)}, bf16[2,16,64,128]{3,2,1,0:T(8,128)(2,1)S(1)}, u32[]{:S(2)}, u32[]{:S(2)}) collective-permute-start(bf16[2,16,64,128]{3,2,1,0:T(8,128)(2,1)S(1)} %fusion.16), channel_id=1, source_target_pairs={{0,8},{1,9},{2,10},{3,11},{4,12},{5,13},{6,14},{7,15},{8,0},{9,1},... | collective-permute-start | bytes 1572872 | tf_op jit(solution)/shard_map/ppermute | solution.py:15
  488.6 11.6 %slice-start = ((s8[7340032]{0:T(1024)(128)(4,1)}), s8[4194304]{0:T(1024)(128)(4,1)S(1)}, s32[]{:S(2)}) async-start(s8[7340032]{0:T(1024)(128)(4,1)} %bitcast.564), calls=%async_computation | async-start | bytes 8388608
  489.3 21.2 %collective-permute-start.14 = (bf16[2,16,64,128]{3,2,1,0:T(8,128)(2,1)S(1)}, bf16[2,16,64,128]{3,2,1,0:T(8,128)(2,1)S(1)}, u32[]{:S(2)}, u32[]{:S(2)}) collective-permute-start(bf16[2,16,64,128]{3,2,1,0:T(8,128)(2,1)S(1)} %fusion.22), channel_id=1, source_target_pairs={{0,8},{1,9},{2,10},{3,11},{4,12},{5,13},{6,14},{7,15},{8,0},{9,1},... | collective-permute-start | bytes 1572872 | tf_op jit(solution)/shard_map/ppermute | solution.py:15
  499.2 1.9 slice-start.1
  501.3 21.2 %collective-permute-start.21 = (bf16[2,16,64,128]{3,2,1,0:T(8,128)(2,1)S(1)}, bf16[2,16,64,128]{3,2,1,0:T(8,128)(2,1)S(1)}, u32[]{:S(2)}, u32[]{:S(2)}) collective-permute-start(bf16[2,16,64,128]{3,2,1,0:T(8,128)(2,1)S(1)} %fusion.15), channel_id=1, source_target_pairs={{0,4},{1,5},{2,6},{3,7},{4,0},{5,1},{6,2},{7,3},{8,12},{9,13},{10,... | collective-permute-start | bytes 1572872 | tf_op jit(solution)/shard_map/ppermute | solution.py:15
  511.6 35.1 %collective-permute-start.15 = (bf16[2,16,64,128]{3,2,1,0:T(8,128)(2,1)S(1)}, bf16[2,16,64,128]{3,2,1,0:T(8,128)(2,1)S(1)}, u32[]{:S(2)}, u32[]{:S(2)}) collective-permute-start(bf16[2,16,64,128]{3,2,1,0:T(8,128)(2,1)S(1)} %fusion.21), channel_id=1, source_target_pairs={{0,4},{1,5},{2,6},{3,7},{4,0},{5,1},{6,2},{7,3},{8,12},{9,13},{10,... | collective-permute-start | bytes 1572872 | tf_op jit(solution)/shard_map/ppermute | solution.py:15
  523.6 66.2 %collective-permute-start.22 = (bf16[2,16,64,128]{3,2,1,0:T(8,128)(2,1)S(1)}, bf16[2,16,64,128]{3,2,1,0:T(8,128)(2,1)S(1)}, u32[]{:S(2)}, u32[]{:S(2)}) collective-permute-start(bf16[2,16,64,128]{3,2,1,0:T(8,128)(2,1)S(1)} %fusion.14), channel_id=1, source_target_pairs={{0,2},{1,3},{2,0},{3,1},{4,6},{5,7},{6,4},{7,5},{8,10},{9,11},{10,... | collective-permute-start | bytes 1572872 | tf_op jit(solution)/shard_map/ppermute | solution.py:15
  547.9 53.3 %collective-permute-start.16 = (bf16[2,16,64,128]{3,2,1,0:T(8,128)(2,1)S(1)}, bf16[2,16,64,128]{3,2,1,0:T(8,128)(2,1)S(1)}, u32[]{:S(2)}, u32[]{:S(2)}) collective-permute-start(bf16[2,16,64,128]{3,2,1,0:T(8,128)(2,1)S(1)} %fusion.20), channel_id=1, source_target_pairs={{0,2},{1,3},{2,0},{3,1},{4,6},{5,7},{6,4},{7,5},{8,10},{9,11},{10,... | collective-permute-start | bytes 1572872 | tf_op jit(solution)/shard_map/ppermute | solution.py:15
  591.0 21.3 %collective-permute-start.23 = (bf16[2,16,64,128]{3,2,1,0:T(8,128)(2,1)S(1)}, bf16[2,16,64,128]{3,2,1,0:T(8,128)(2,1)S(1)}, u32[]{:S(2)}, u32[]{:S(2)}) collective-permute-start(bf16[2,16,64,128]{3,2,1,0:T(8,128)(2,1)S(1)} %fusion.13), channel_id=1, source_target_pairs={{0,1},{1,0},{2,3},{3,2},{4,5},{5,4},{6,7},{7,6},{8,9},{9,8},{10,11... | collective-permute-start | bytes 1572872 | tf_op jit(solution)/shard_map/ppermute | solution.py:15
  602.3 21.2 %collective-permute-start.17 = (bf16[2,16,64,128]{3,2,1,0:T(8,128)(2,1)S(1)}, bf16[2,16,64,128]{3,2,1,0:T(8,128)(2,1)S(1)}, u32[]{:S(2)}, u32[]{:S(2)}) collective-permute-start(bf16[2,16,64,128]{3,2,1,0:T(8,128)(2,1)S(1)} %fusion.19), channel_id=1, source_target_pairs={{0,1},{1,0},{2,3},{3,2},{4,5},{5,4},{6,7},{7,6},{8,9},{9,8},{10,11... | collective-permute-start | bytes 1572872 | tf_op jit(solution)/shard_map/ppermute | solution.py:15
  612.7 12.2 %copy-start.1 = (bf16[2,64,2048]{2,1,0:T(8,128)(2,1)S(1)}, bf16[2,64,2048]{2,1,0:T(8,128)(2,1)}, u32[]{:S(2)}) copy-start(bf16[2,64,2048]{2,1,0:T(8,128)(2,1)} %param.8) | copy-start | bytes 1572868
